TPU v7x, 256 devices: a whole 4x4x8 slice. The times are simulated.
256 devices in a mesh: grp: 8 (over y, core), sub: 32 (over x, z).
Axes of the slice: x: 4, y: 4, z: 8, core: 2. Of those that a mesh axis runs over, the one named last changes fastest.
Arguments:
- cluster_pos: float32 [3, 4096], P(None, 'sub'), may hold values from -3 to 3
- cluster_vel: float32 [3, 4096], P(None, 'sub'), may hold values from -15 to 15
- cluster_mass: float32 [4096], P('sub'), may hold values from 3 to 60
- galaxy_pos: float32 [3, 131072], P(None, ('grp', 'sub')), may hold values from -1 to 7
- galaxy_vel: float32 [3, 131072], P(None, ('grp', 'sub')), may hold values from -3 to 3
- galaxy_kind: int32 [131072], P(('grp', 'sub')), may hold values from 0 to 3
- species_mass: float32 [4], replicated, may hold values from 10 to 80
Outputs:
- cluster_pos_out: float32 [3, 4096], P(None, 'sub')
- cluster_vel_out: float32 [3, 4096], P(None, 'sub')
- galaxy_pos_out: float32 [3, 131072], P(None, ('grp', 'sub'))
- galaxy_vel_out: float32 [3, 131072], P(None, ('grp', 'sub'))
All inputs are finite; a program needn't handle non-finite values.
Results may differ from a plain program's by a relative error of at most 0.0003.
Values sent between devices are 32-bit elements; how exact they have to be, the bound alone decides.
A program may use at most 64 MiB of HBM per device.

v0:
```python
import jax
import jax.numpy as jnp
from jax import lax
from jax.sharding import PartitionSpec as P

SUBSTEPS = 8
step_time = 0.5
bridge_soft = 0.01
cluster_soft = 0.0025
tile_limit = 524288


def pick_block(target_count, source_count):
    tile_size = target_count
    while tile_size > 1 and (
        tile_size * source_count > tile_limit or target_count % tile_size != 0
    ):
        tile_size = tile_size // 2
    return tile_size


def field(targets, sources, masses, soften):
    target_count = targets.shape[1]
    tile_size = pick_block(target_count, sources.shape[1])

    def field_one_tile(target_tile):
        separation = sources[:, None, :] - target_tile[:, :, None]
        distance = jnp.sum(separation * separation, axis=0) + soften
        inverse = lax.rsqrt(distance)
        weight = masses[None, :] * inverse * inverse * inverse
        return jnp.sum(separation * weight[None], axis=2)

    stacked = targets.reshape(3, target_count // tile_size, tile_size).transpose(1, 0, 2)
    result = lax.map(field_one_tile, stacked)
    return result.transpose(1, 0, 2).reshape(3, target_count)


def rates(target_pos, target_vel, source_pos, source_vel, masses, soften):
    target_count = target_pos.shape[1]
    tile_size = pick_block(target_count, source_pos.shape[1])

    def rates_one_tile(target_tile):
        separation = source_pos[:, None, :] - target_tile[:3, :, None]
        closing = source_vel[:, None, :] - target_tile[3:, :, None]
        distance = jnp.sum(separation * separation, axis=0) + soften
        inverse = lax.rsqrt(distance)
        weight = masses[None, :] * inverse * inverse * inverse
        radial = 3.0 * jnp.sum(separation * closing, axis=0) / distance
        acceleration = jnp.sum(separation * weight[None], axis=2)
        jerk_rate = jnp.sum((closing - radial[None] * separation) * weight[None], axis=2)
        return jnp.concatenate([acceleration, jerk_rate], axis=0)

    stacked = jnp.concatenate([target_pos, target_vel], axis=0)
    stacked = stacked.reshape(6, target_count // tile_size, tile_size).transpose(1, 0, 2)
    result = lax.map(rates_one_tile, stacked)
    return result.transpose(1, 0, 2).reshape(6, target_count)


def local(
    cluster_pos, cluster_vel, cluster_mass, galaxy_pos, galaxy_vel, galaxy_kind, species_mass
):
    star_count = cluster_pos.shape[1]
    member_count = lax.axis_size("sub")
    group_count = lax.axis_size("grp")
    total_stars = star_count * member_count
    total_bodies = galaxy_pos.shape[1] * member_count * group_count
    star_mass = cluster_mass / total_stars
    species = jnp.arange(species_mass.shape[0], dtype=jnp.int32)
    body_mass = (
        jnp.sum(
            jnp.where(galaxy_kind[None, :] == species[:, None], species_mass[:, None], 0.0), axis=0
        )
        / total_bodies
    )
    half_step = step_time / 2.0

    def kick(star_positions, body_positions):
        stacked = jnp.concatenate([star_positions, star_mass[None, :]], axis=0)
        gathered = lax.all_gather(stacked, "sub", axis=1, tiled=True)
        galaxy_push = field(body_positions, gathered[:3], gathered[3], bridge_soft)
        partial_value = field(gathered[:3], body_positions, body_mass, bridge_soft)
        summed = lax.psum(partial_value, ("grp", "sub"))
        cluster_pull = lax.dynamic_slice_in_dim(
            summed, lax.axis_index("sub") * star_count, star_count, 1
        )
        return (cluster_pull, galaxy_push)

    def evaluate(guess_pos, guess_vel):
        sources = jnp.concatenate([guess_pos, guess_vel, star_mass[None, :]], axis=0)
        target_pos, target_vel = (guess_pos, guess_vel)
        source_piece = lax.all_gather(sources, "sub", axis=1, tiled=True)
        result = rates(
            target_pos,
            target_vel,
            source_piece[:3],
            source_piece[3:6],
            source_piece[6],
            cluster_soft,
        )
        return (result[:3], result[3:])

    first_pull, first_push = kick(cluster_pos, galaxy_pos)
    star_vel = cluster_vel + half_step * first_pull
    body_vel = galaxy_vel + half_step * first_push
    body_pos = galaxy_pos + step_time * body_vel
    substep_time = step_time / SUBSTEPS
    positions, velocity = (cluster_pos, star_vel)
    acceleration, jerk_rate = evaluate(positions, velocity)
    for substep in range(SUBSTEPS):
        guess_pos = positions + substep_time * (
            velocity + substep_time * (acceleration / 2.0 + substep_time * jerk_rate / 6.0)
        )
        guess_vel = velocity + substep_time * (acceleration + substep_time * jerk_rate / 2.0)
        new_acc, new_jerk = evaluate(guess_pos, guess_vel)
        new_vel = (
            velocity
            + substep_time / 2.0 * (acceleration + new_acc)
            + substep_time * substep_time / 12.0 * (jerk_rate - new_jerk)
        )
        new_pos = (
            positions
            + substep_time / 2.0 * (velocity + new_vel)
            + substep_time * substep_time / 12.0 * (acceleration - new_acc)
        )
        positions, velocity, acceleration, jerk_rate = (new_pos, new_vel, new_acc, new_jerk)
    second_pull, second_push = kick(positions, body_pos)
    return (
        positions,
        velocity + half_step * second_pull,
        body_pos,
        body_vel + half_step * second_push,
    )


def solution(mesh):
    return jax.shard_map(
        local,
        mesh=mesh,
        in_specs=(
            P(None, "sub"),
            P(None, "sub"),
            P("sub"),
            P(None, ("grp", "sub")),
            P(None, ("grp", "sub")),
            P(("grp", "sub")),
            P(),
        ),
        out_specs=(
            P(None, "sub"),
            P(None, "sub"),
            P(None, ("grp", "sub")),
            P(None, ("grp", "sub")),
        ),
        check_vma=False,
    )
```

profile of v0, /device:TPU:1, one launch (start us, length us, event | category | flops | bytes accessed | tf_op | source)
XLA Modules:
  0.0 715.4 jit_solution(4176489332510097580)
XLA Ops:
  2.0 40.5 %all_gather.33 = f32[4,4096]{1,0:T(4,128)S(1)} all-gather(f32[4,128]{1,0:T(4,128)S(1)} %pad_maximum_fusion.10), channel_id=1, replica_groups=mesh['grp'=8,'sub'=32] {'sub'}, dimensions={1}, use_global_device_ids=true | all-gather | bytes 67584 | tf_op jit(solution)/shard_map/all_gather | solution.py:79
  43.3 14.5 %while.8 = (s32[]{:T(128)}, f32[4,3,1024]{2,1,0:T(4,128)S(1)}, f32[3,512]{1,0:T(4,128)}, f32[4,3,1024]{2,1,0:T(4,128)S(1)}, f32[512]{0:T(512)S(1)}, /*index=5*/s32[]{:T(128)}) while((s32[]{:T(128)}, f32[4,3,1024]{2,1,0:T(4,128)S(1)}, f32[3,512]{1,0:T(4,128)}, f32[4,3,1024]{2,1,0:T(4,128)S(1)}, f32[512]{0:T(512)S(1)}, ...), condition=%wide.region_4.5_spmd, body=%wide.region_1.4_spmd.sunk | while | flops 11006978 | bytes 8521833 | solution.py:34
  57.8 87.6 %psum.14 = f32[3,4096]{1,0:T(4,128)S(1)} all-reduce(f32[3,4096]{1,0:T(4,128)S(1)} %bitcast.93), channel_id=1, replica_groups=mesh['grp'=8,'sub'=32] {'grp','sub'}, use_global_device_ids=true, to_apply=%region_5.6 | all-reduce | flops 12288 | bytes 98304 | tf_op jit(solution)/shard_map/psum | solution.py:82
  145.4 31.0 %all_gather.34 = f32[7,4096]{1,0:T(8,128)S(1)} all-gather(f32[7,128]{1,0:T(8,128)S(1)} %pad_maximum_fusion.8), channel_id=1, replica_groups=mesh['grp'=8,'sub'=32] {'sub'}, dimensions={1}, use_global_device_ids=true | all-gather | bytes 118272 | tf_op jit(solution)/shard_map/all_gather | solution.py:91
  181.2 32.3 %all_gather.35 = f32[7,4096]{1,0:T(8,128)S(1)} all-gather(f32[7,128]{1,0:T(8,128)S(1)} %pad_maximum_fusion.7), channel_id=1, replica_groups=mesh['grp'=8,'sub'=32] {'sub'}, dimensions={1}, use_global_device_ids=true | all-gather | bytes 118272 | tf_op jit(solution)/shard_map/all_gather | solution.py:91
  216.2 2.2 fusion.11
  218.4 31.8 %all_gather.36 = f32[7,4096]{1,0:T(8,128)S(1)} all-gather(f32[7,128]{1,0:T(8,128)S(1)} %pad_maximum_fusion.6), channel_id=1, replica_groups=mesh['grp'=8,'sub'=32] {'sub'}, dimensions={1}, use_global_device_ids=true | all-gather | bytes 118272 | tf_op jit(solution)/shard_map/all_gather | solution.py:91
  252.9 2.2 fusion.13
  255.1 33.7 %all_gather.37 = f32[7,4096]{1,0:T(8,128)S(1)} all-gather(f32[7,128]{1,0:T(8,128)S(1)} %pad_maximum_fusion.5), channel_id=1, replica_groups=mesh['grp'=8,'sub'=32] {'sub'}, dimensions={1}, use_global_device_ids=true | all-gather | bytes 118272 | tf_op jit(solution)/shard_map/all_gather | solution.py:91
  291.5 2.2 fusion.15
  293.7 30.9 %all_gather.38 = f32[7,4096]{1,0:T(8,128)S(1)} all-gather(f32[7,128]{1,0:T(8,128)S(1)} %pad_maximum_fusion.4), channel_id=1, replica_groups=mesh['grp'=8,'sub'=32] {'sub'}, dimensions={1}, use_global_device_ids=true | all-gather | bytes 118272 | tf_op jit(solution)/shard_map/all_gather | solution.py:91
  327.3 2.2 fusion.17
  329.5 33.5 %all_gather.39 = f32[7,4096]{1,0:T(8,128)S(1)} all-gather(f32[7,128]{1,0:T(8,128)S(1)} %pad_maximum_fusion.3), channel_id=1, replica_groups=mesh['grp'=8,'sub'=32] {'sub'}, dimensions={1}, use_global_device_ids=true | all-gather | bytes 118272 | tf_op jit(solution)/shard_map/all_gather | solution.py:91
  365.7 2.2 fusion.19
  367.9 30.7 %all_gather.40 = f32[7,4096]{1,0:T(8,128)S(1)} all-gather(f32[7,128]{1,0:T(8,128)S(1)} %pad_maximum_fusion.2), channel_id=1, replica_groups=mesh['grp'=8,'sub'=32] {'sub'}, dimensions={1}, use_global_device_ids=true | all-gather | bytes 118272 | tf_op jit(solution)/shard_map/all_gather | solution.py:91
  401.3 2.2 fusion.21
  403.5 33.4 %all_gather.41 = f32[7,4096]{1,0:T(8,128)S(1)} all-gather(f32[7,128]{1,0:T(8,128)S(1)} %pad_maximum_fusion.1), channel_id=1, replica_groups=mesh['grp'=8,'sub'=32] {'sub'}, dimensions={1}, use_global_device_ids=true | all-gather | bytes 118272 | tf_op jit(solution)/shard_map/all_gather | solution.py:91
  439.6 2.2 fusion.23
  441.8 31.1 %all_gather.42 = f32[7,4096]{1,0:T(8,128)S(1)} all-gather(f32[7,128]{1,0:T(8,128)S(1)} %pad_maximum_fusion), channel_id=1, replica_groups=mesh['grp'=8,'sub'=32] {'sub'}, dimensions={1}, use_global_device_ids=true | all-gather | bytes 118272 | tf_op jit(solution)/shard_map/all_gather | solution.py:91
  477.9 36.5 %all_gather.43 = f32[4,4096]{1,0:T(4,128)S(1)} all-gather(f32[4,128]{1,0:T(4,128)S(1)} %pad_maximum_fusion.9), channel_id=1, replica_groups=mesh['grp'=8,'sub'=32] {'sub'}, dimensions={1}, use_global_device_ids=true | all-gather | bytes 67584 | tf_op jit(solution)/shard_map/all_gather | solution.py:79
  514.4 8.5 %while.9 = (s32[]{:T(128)}, f32[4,3,128]{2,1,0:T(4,128)S(1)}, f32[3,4096]{1,0:T(4,128)S(1)}, f32[4,3,128]{2,1,0:T(4,128)S(1)}, f32[1,4096]{1,0:T(1,128)S(1)}, /*index=5*/s32[]{:T(128)}) while((s32[]{:T(128)}, f32[4,3,128]{2,1,0:T(4,128)S(1)}, f32[3,4096]{1,0:T(4,128)S(1)}, f32[4,3,128]{2,1,0:T(4,128)S(1)}, f32[1,4096]{1,0:T(1,128)S(1)}, ...), condition=%wide.region_45.46_spmd, body=%wide.region_42.45_spmd.sunk | while | flops 11009666 | bytes 8515149 | solution.py:34
  523.0 8.5 %while.11 = (s32[]{:T(128)}, f32[4,3,128]{2,1,0:T(4,128)S(1)}, f32[3,4096]{1,0:T(4,128)S(1)}, f32[4,3,128]{2,1,0:T(4,128)S(1)}, f32[1,4096]{1,0:T(1,128)S(1)}, /*index=5*/s32[]{:T(128)}) while((s32[]{:T(128)}, f32[4,3,128]{2,1,0:T(4,128)S(1)}, f32[3,4096]{1,0:T(4,128)S(1)}, f32[4,3,128]{2,1,0:T(4,128)S(1)}, f32[1,4096]{1,0:T(1,128)S(1)}, ...), condition=%wide.region_54.55_spmd, body=%wide.region_51.54_spmd.sunk | while | flops 11009666 | bytes 8515149 | solution.py:34
  532.1 10.4 %while.10 = (s32[]{:T(128)}, f32[4,3,1024]{2,1,0:T(4,128)S(1)}, f32[3,512]{1,0:T(4,128)S(1)}, f32[4,3,1024]{2,1,0:T(4,128)S(1)}, f32[512]{0:T(512)S(1)}, /*index=5*/s32[]{:T(128)}) while((s32[]{:T(128)}, f32[4,3,1024]{2,1,0:T(4,128)S(1)}, f32[3,512]{1,0:T(4,128)S(1)}, f32[4,3,1024]{2,1,0:T(4,128)S(1)}, f32[512]{0:T(512)S(1)}, ...), condition=%wide.region_49.50_spmd, body=%wide.region_46.49_spmd.sunk | while | flops 11006978 | bytes 8497229 | solution.py:34
  542.5 171.9 %psum.15 = f32[3,4096]{1,0:T(4,128)S(1)} all-reduce(f32[3,4096]{1,0:T(4,128)S(1)} %bitcast.92), channel_id=1, replica_groups=mesh['grp'=8,'sub'=32] {'grp','sub'}, use_global_device_ids=true, to_apply=%region_50.51 | all-reduce | flops 12288 | bytes 98304 | tf_op jit(solution)/shard_map/psum | solution.py:82
  (174 shorter events, 72.9 us)
Async XLA Ops:
  43.2 102.1 %copy-start.6 = (f32[3,128]{1,0:T(4,128)S(1)}, f32[3,128]{1,0:T(4,128)}, u32[]{:S(2)}) copy-start(f32[3,128]{1,0:T(4,128)} %param.16) | copy-start | bytes 4612
  43.2 102.1 %copy-start.3 = (f32[3,128]{1,0:T(4,128)S(1)}, f32[3,128]{1,0:T(4,128)}, u32[]{:S(2)}) copy-start(f32[3,128]{1,0:T(4,128)} %param.15) | copy-start | bytes 4612
  44.9 0.7 copy-start
  48.6 0.7 copy-start
  52.2 0.7 copy-start
  55.8 0.7 copy-start
  475.6 38.8 %copy-start.1 = (f32[3,512]{1,0:T(4,128)S(1)}, f32[3,512]{1,0:T(4,128)}, u32[]{:S(2)}) copy-start(f32[3,512]{1,0:T(4,128)} %get-tuple-element.607) | copy-start | bytes 18436
  477.8 36.6 %copy-start.5 = (f32[3,128]{1,0:T(4,128)}, f32[3,128]{1,0:T(4,128)S(1)}, u32[]{:S(2)}) copy-start(f32[3,128]{1,0:T(4,128)S(1)} %multiply_add_fusion.2) | copy-start | bytes 4612
  514.4 8.5 %copy-start.4 = (f32[3,512]{1,0:T(4,128)S(1)}, f32[3,512]{1,0:T(4,128)}, u32[]{:S(2)}) copy-start(f32[3,512]{1,0:T(4,128)} %param.19) | copy-start | bytes 18436
  542.5 172.5 %copy-start.2 = (f32[3,512]{1,0:T(4,128)}, f32[3,512]{1,0:T(4,128)S(1)}, u32[]{:S(2)}) copy-start(f32[3,512]{1,0:T(4,128)S(1)} %get-tuple-element.610) | copy-start | bytes 18436
where the time goes:
time: 725 us; the launch traced here: 715 us
  blocking collectives  625 us (86%)
  other arithmetic  86 us (12%)
    all_gather x9, blocking collectives, evaluate(): source_piece = lax.all_gather(sources, 'sub', axis=1, tiled=True)  288 us
    psum x2, blocking collectives, kick(): summed = lax.psum(partial_value, ('grp', 'sub'))  259 us
    all_gather x2, blocking collectives, kick(): gathered = lax.all_gather(stacked, 'sub', axis=1, tiled=True)  76.9 us
    reduce_sum x8, other arithmetic, rates_one_tile(): jnp.sum((closing - radial[None] * separation) * weight[None], axis=2)  17.5 us
    reduce_sum x16, other arithmetic, field_one_tile(): distance = jnp.sum(separation * separation, axis=0) + soften  17.3 us
    reduce_sum x16, other arithmetic, field_one_tile(): return jnp.sum(separation * weight[None], axis=2)  16.5 us
    reduce_sum x8, other arithmetic, rates_one_tile(): radial = 3.0 * jnp.sum(separation * closing, axis=0) / distance  16.4 us

commit v1 on v0

--- a/solution.py
+++ b/solution.py
@@ -76,7 +76,7 @@
 
     def kick(star_positions, body_positions):
         stacked = jnp.concatenate([star_positions, star_mass[None, :]], axis=0)
-        gathered = lax.all_gather(stacked, "sub", axis=1, tiled=True)
+        gathered = jnp.concatenate(lax.all_gather(stacked, "sub"), axis=1)
         galaxy_push = field(body_positions, gathered[:3], gathered[3], bridge_soft)
         partial_value = field(gathered[:3], body_positions, body_mass, bridge_soft)
         summed = lax.psum(partial_value, ("grp", "sub"))

time: 725 us -> 727 us (level)
  no operation moved by 1% of the time
where the time goes in v1:
time: 727 us; the launch traced here: 719 us
  blocking collectives  625 us (86%)
  other arithmetic  86.7 us (12%)
    all_gather x9, blocking collectives, evaluate(): source_piece = lax.all_gather(sources, 'sub', axis=1, tiled=True)  289 us
    psum x2, blocking collectives, kick(): summed = lax.psum(partial_value, ('grp', 'sub'))  261 us
    all_gather x2, blocking collectives, kick(): gathered = jnp.concatenate(lax.all_gather(stacked, 'sub'), axis=1)  74.7 us
    reduce_sum x8, other arithmetic, rates_one_tile(): jnp.sum((closing - radial[None] * separation) * weight[None], axis=2)  17.5 us
    reduce_sum x16, other arithmetic, field_one_tile(): distance = jnp.sum(separation * separation, axis=0) + soften  17.3 us
    reduce_sum x16, other arithmetic, field_one_tile(): return jnp.sum(separation * weight[None], axis=2)  16.5 us
    reduce_sum x8, other arithmetic, rates_one_tile(): radial = 3.0 * jnp.sum(separation * closing, axis=0) / distance  16.4 us

profile of v1, /device:TPU:1, one launch (start us, length us, event | category | flops | bytes accessed | tf_op | source)
XLA Modules:
  0.0 719.3 jit_solution(8340239563741090129)
XLA Ops:
  2.8 40.5 %all-gather.2 = f32[32,4,128]{2,1,0:T(4,128)S(1)} all-gather(f32[1,4,128]{2,1,0:T(4,128)S(1)} %fusion.53), channel_id=2, replica_groups=mesh['grp'=8,'sub'=32] {'sub'}, dimensions={0}, use_global_device_ids=true | all-gather | bytes 67584 | tf_op jit(solution)/shard_map/all_gather | solution.py:79
  43.3 14.5 %while.8 = (s32[]{:T(128)}, f32[4,3,1024]{2,1,0:T(4,128)S(1)}, f32[3,512]{1,0:T(4,128)}, f32[4,3,1024]{2,1,0:T(4,128)S(1)}, f32[512]{0:T(512)S(1)}, /*index=5*/s32[]{:T(128)}) while((s32[]{:T(128)}, f32[4,3,1024]{2,1,0:T(4,128)S(1)}, f32[3,512]{1,0:T(4,128)}, f32[4,3,1024]{2,1,0:T(4,128)S(1)}, f32[512]{0:T(512)S(1)}, ...), condition=%wide.region_4.5_spmd, body=%wide.region_1.4_spmd.sunk | while | flops 11006978 | bytes 8521841 | solution.py:34
  57.8 87.6 %psum.14 = f32[3,4096]{1,0:T(4,128)S(1)} all-reduce(f32[3,4096]{1,0:T(4,128)S(1)} %bitcast.105), channel_id=1, replica_groups=mesh['grp'=8,'sub'=32] {'grp','sub'}, use_global_device_ids=true, to_apply=%region_5.6 | all-reduce | flops 12288 | bytes 98304 | tf_op jit(solution)/shard_map/psum | solution.py:82
  145.4 11.2 %while.9 = (s32[]{:T(128)}, f32[4,3,128]{2,1,0:T(4,128)S(1)}, f32[3,4096]{1,0:T(4,128)S(1)}, f32[4,3,128]{2,1,0:T(4,128)}, f32[1,4096]{1,0:T(1,128)S(1)}, /*index=5*/s32[]{:T(128)}) while((s32[]{:T(128)}, f32[4,3,128]{2,1,0:T(4,128)S(1)}, f32[3,4096]{1,0:T(4,128)S(1)}, f32[4,3,128]{2,1,0:T(4,128)}, f32[1,4096]{1,0:T(1,128)S(1)}, ...), condition=%wide.region_45.46_spmd, body=%wide.region_42.45_spmd.sunk | while | flops 11009666 | bytes 8515157 | solution.py:34
  157.4 31.0 %all_gather.41 = f32[7,4096]{1,0:T(8,128)S(1)} all-gather(f32[7,128]{1,0:T(8,128)S(1)} %pad_maximum_fusion.8), channel_id=1, replica_groups=mesh['grp'=8,'sub'=32] {'sub'}, dimensions={1}, use_global_device_ids=true | all-gather | bytes 118272 | tf_op jit(solution)/shard_map/all_gather | solution.py:91
  193.1 32.9 %all_gather.42 = f32[7,4096]{1,0:T(8,128)S(1)} all-gather(f32[7,128]{1,0:T(8,128)S(1)} %pad_maximum_fusion.7), channel_id=1, replica_groups=mesh['grp'=8,'sub'=32] {'sub'}, dimensions={1}, use_global_device_ids=true | all-gather | bytes 118272 | tf_op jit(solution)/shard_map/all_gather | solution.py:91
  228.7 2.2 fusion.11
  230.9 31.3 %all_gather.43 = f32[7,4096]{1,0:T(8,128)S(1)} all-gather(f32[7,128]{1,0:T(8,128)S(1)} %pad_maximum_fusion.6), channel_id=1, replica_groups=mesh['grp'=8,'sub'=32] {'sub'}, dimensions={1}, use_global_device_ids=true | all-gather | bytes 118272 | tf_op jit(solution)/shard_map/all_gather | solution.py:91
  264.9 2.2 fusion.13
  267.1 33.8 %all_gather.44 = f32[7,4096]{1,0:T(8,128)S(1)} all-gather(f32[7,128]{1,0:T(8,128)S(1)} %pad_maximum_fusion.5), channel_id=1, replica_groups=mesh['grp'=8,'sub'=32] {'sub'}, dimensions={1}, use_global_device_ids=true | all-gather | bytes 118272 | tf_op jit(solution)/shard_map/all_gather | solution.py:91
  303.6 2.2 fusion.15
  305.8 30.5 %all_gather.45 = f32[7,4096]{1,0:T(8,128)S(1)} all-gather(f32[7,128]{1,0:T(8,128)S(1)} %pad_maximum_fusion.4), channel_id=1, replica_groups=mesh['grp'=8,'sub'=32] {'sub'}, dimensions={1}, use_global_device_ids=true | all-gather | bytes 118272 | tf_op jit(solution)/shard_map/all_gather | solution.py:91
  339.0 2.2 fusion.17
  341.3 33.2 %all_gather.46 = f32[7,4096]{1,0:T(8,128)S(1)} all-gather(f32[7,128]{1,0:T(8,128)S(1)} %pad_maximum_fusion.3), channel_id=1, replica_groups=mesh['grp'=8,'sub'=32] {'sub'}, dimensions={1}, use_global_device_ids=true | all-gather | bytes 118272 | tf_op jit(solution)/shard_map/all_gather | solution.py:91
  377.1 2.2 fusion.19
  379.3 31.3 %all_gather.47 = f32[7,4096]{1,0:T(8,128)S(1)} all-gather(f32[7,128]{1,0:T(8,128)S(1)} %pad_maximum_fusion.2), channel_id=1, replica_groups=mesh['grp'=8,'sub'=32] {'sub'}, dimensions={1}, use_global_device_ids=true | all-gather | bytes 118272 | tf_op jit(solution)/shard_map/all_gather | solution.py:91
  413.3 2.2 fusion.21
  415.6 32.4 %all_gather.48 = f32[7,4096]{1,0:T(8,128)S(1)} all-gather(f32[7,128]{1,0:T(8,128)S(1)} %pad_maximum_fusion.1), channel_id=1, replica_groups=mesh['grp'=8,'sub'=32] {'sub'}, dimensions={1}, use_global_device_ids=true | all-gather | bytes 118272 | tf_op jit(solution)/shard_map/all_gather | solution.py:91
  450.7 2.2 fusion.23
  452.9 32.9 %all_gather.49 = f32[7,4096]{1,0:T(8,128)S(1)} all-gather(f32[7,128]{1,0:T(8,128)S(1)} %pad_maximum_fusion), channel_id=1, replica_groups=mesh['grp'=8,'sub'=32] {'sub'}, dimensions={1}, use_global_device_ids=true | all-gather | bytes 118272 | tf_op jit(solution)/shard_map/all_gather | solution.py:91
  490.7 34.2 %all-gather.3 = f32[32,4,128]{2,1,0:T(4,128)S(1)} all-gather(f32[1,4,128]{2,1,0:T(4,128)S(1)} %fusion.54), channel_id=3, replica_groups=mesh['grp'=8,'sub'=32] {'sub'}, dimensions={0}, use_global_device_ids=true | all-gather | bytes 67584 | tf_op jit(solution)/shard_map/all_gather | solution.py:79
  525.0 10.4 %while.10 = (s32[]{:T(128)}, f32[4,3,1024]{2,1,0:T(4,128)S(1)}, f32[3,512]{1,0:T(4,128)S(1)}, f32[4,3,1024]{2,1,0:T(4,128)S(1)}, f32[512]{0:T(512)S(1)}, /*index=5*/s32[]{:T(128)}) while((s32[]{:T(128)}, f32[4,3,1024]{2,1,0:T(4,128)S(1)}, f32[3,512]{1,0:T(4,128)S(1)}, f32[4,3,1024]{2,1,0:T(4,128)S(1)}, f32[512]{0:T(512)S(1)}, ...), condition=%wide.region_49.50_spmd, body=%wide.region_46.49_spmd.sunk | while | flops 11006978 | bytes 8497237 | solution.py:34
  535.4 173.7 %psum.15 = f32[3,4096]{1,0:T(4,128)S(1)} all-reduce(f32[3,4096]{1,0:T(4,128)S(1)} %bitcast.106), channel_id=1, replica_groups=mesh['grp'=8,'sub'=32] {'grp','sub'}, use_global_device_ids=true, to_apply=%region_50.51 | all-reduce | flops 12288 | bytes 98304 | tf_op jit(solution)/shard_map/psum | solution.py:82
  709.7 8.5 %while.11 = (s32[]{:T(128)}, f32[4,3,128]{2,1,0:T(4,128)S(1)}, f32[3,4096]{1,0:T(4,128)S(1)}, f32[4,3,128]{2,1,0:T(4,128)S(1)}, f32[1,4096]{1,0:T(1,128)S(1)}, /*index=5*/s32[]{:T(128)}) while((s32[]{:T(128)}, f32[4,3,128]{2,1,0:T(4,128)S(1)}, f32[3,4096]{1,0:T(4,128)S(1)}, f32[4,3,128]{2,1,0:T(4,128)S(1)}, f32[1,4096]{1,0:T(1,128)S(1)}, ...), condition=%wide.region_54.55_spmd, body=%wide.region_51.54_spmd.sunk | while | flops 11009666 | bytes 8515157 | solution.py:34
  (174 shorter events, 76.4 us)
Async XLA Ops:
  43.3 102.1 %copy-start.5 = (f32[3,128]{1,0:T(4,128)S(1)}, f32[3,128]{1,0:T(4,128)}, u32[]{:S(2)}) copy-start(f32[3,128]{1,0:T(4,128)} %param.16) | copy-start | bytes 4612
  45.0 0.7 copy-start
  48.6 0.7 copy-start
  52.2 0.7 copy-start
  55.9 0.7 copy-start
  145.4 11.2 %copy-start.2 = (f32[3,128]{1,0:T(4,128)S(1)}, f32[3,128]{1,0:T(4,128)}, u32[]{:S(2)}) copy-start(f32[3,128]{1,0:T(4,128)} %param.15) | copy-start | bytes 4612
  145.4 11.2 %copy-start.3 = (f32[3,512]{1,0:T(4,128)S(1)}, f32[3,512]{1,0:T(4,128)}, u32[]{:S(2)}) copy-start(f32[3,512]{1,0:T(4,128)} %param.19) | copy-start | bytes 18436
  490.7 34.3 %copy-start.4 = (f32[3,128]{1,0:T(4,128)}, f32[3,128]{1,0:T(4,128)S(1)}, u32[]{:S(2)}) copy-start(f32[3,128]{1,0:T(4,128)S(1)} %multiply_add_fusion.2) | copy-start | bytes 4612
  718.2 0.6 copy-start.1
